TPU v7x, 512 devices: a whole 4x8x8 slice. The times are simulated.
512 devices in a mesh: ctx: 32 (over y, x), db: 16 (over z, core).
Axes of the slice: x: 4, y: 8, z: 8, core: 2. Of those that a mesh axis runs over, the one named last changes fastest.
Arguments:
- stream: bfloat16 [12288, 4096], P('ctx', 'db'), may hold values from -6 to 6
- history: bfloat16 [8, 12288, 4096], P(None, 'ctx', 'db'), may hold values from -6 to 6
- dwa_weights: float32 [9], replicated, may hold values from -0.5 to 1
- w_query: bfloat16 [4096, 4096], P('ctx', 'db'), may hold values from -0.09375 to 0.09375
- w_out: bfloat16 [4096, 4096], P('db', 'ctx'), may hold values from -0.1875 to 0.1875
- encoded_kv: bfloat16 [16, 24, 128, 2, 4096], P('db', None, 'ctx'), may hold values from -340 to 340
- neighbour_ids: int32 [384], replicated, may hold values from 0 to 383, each once
Outputs:
- block_out: bfloat16 [12288, 4096], P('ctx', 'db')
- dense: bfloat16 [12288, 4096], P('ctx', 'db')
Inputs may be any that keep to these rules, and one draw needn't show every extreme that they name: `neighbour_ids`: each stored neighbour is named by exactly one slot.
All inputs are finite; a program needn't handle non-finite values.
Results may differ from a plain program's by a relative error of at most 0.014.
The roundings to bfloat16 on the way count: a program that leaves them out, or rounds other values in their place, can miss the bound.
Values may be sent and summed in bfloat16 or wider, within the bound.
No kernel may reach another device: no remote copies, remote signals or barrier semaphores. Data moves between devices by JAX's collectives and lax.ppermute only.
A program may use at most 64 MiB of HBM per device.

v0:
```python
import jax
import jax.numpy as jnp
from jax import lax
from jax.sharding import PartitionSpec as P

HDIM = 128
SPAN = 64
NNB = 2


def shifted(block, axis, distance):
    devices = range(lax.axis_size(axis))
    route = [(i - distance, i) for i in devices if i - distance in devices]
    return lax.ppermute(block, axis, route)


def attend(queries, key_rows, value_rows):
    group_count, row_count, width = queries.shape
    head_count = width // HDIM
    query_heads = queries.reshape(group_count, row_count, head_count, HDIM)
    key_heads = key_rows.reshape(group_count, key_rows.shape[1], head_count, HDIM)
    value_heads = value_rows.reshape(group_count, value_rows.shape[1], head_count, HDIM)
    scores = jnp.einsum(
        "gqhd,gkhd->ghqk", query_heads, key_heads, preferred_element_type=jnp.float32
    ) * HDIM ** (-0.5)
    row_max = jnp.max(scores, axis=-1, keepdims=True)
    exponent = jnp.exp(scores - row_max)
    weights = (exponent / jnp.sum(exponent, axis=-1, keepdims=True)).astype(jnp.bfloat16)
    mixed = jnp.einsum("ghqk,gkhd->gqhd", weights, value_heads, preferred_element_type=jnp.float32)
    return mixed.astype(jnp.bfloat16).reshape(group_count, row_count, width)


def on_device(stream, history, dwa_weights, w_query, w_out, encoded_kv, neighbour_ids):
    tok_rows = stream.shape[0]
    local_width = w_query.shape[1]
    spans_here = tok_rows // SPAN
    lead_rows = SPAN - 1
    full_stream = lax.all_gather(stream, "db", axis=1, tiled=True)
    queries = jnp.dot(
        full_stream,
        lax.all_gather(w_query, "ctx", axis=0, tiled=True),
        preferred_element_type=jnp.float32,
    ).astype(jnp.bfloat16)
    out_full = lax.all_gather(w_out, "ctx", axis=1, tiled=True)
    groups_here = lax.all_to_all(encoded_kv, "db", split_axis=4, concat_axis=0, tiled=True)
    slab_rows = encoded_kv.shape[2]
    store = groups_here.reshape(-1, slab_rows, 2, local_width)
    ctx_count = lax.axis_size("ctx")
    row_requests = neighbour_ids.shape[0] // ctx_count
    wanted = neighbour_ids.reshape(ctx_count, row_requests).T
    outgoing = jnp.take(store, wanted, axis=0)
    arrived = lax.all_to_all(outgoing, "ctx", split_axis=1, concat_axis=1, tiled=True)
    neighbours = arrived.reshape(spans_here, NNB * ctx_count * slab_rows, 2, local_width)
    key_rows = neighbours[:, :, 0]
    value_rows = neighbours[:, :, 1]
    carried = shifted(neighbours[spans_here - 1], "ctx", 1)
    all_keys = jnp.concatenate([carried[None, :, 0], key_rows], 0)
    all_values = jnp.concatenate([carried[None, :, 1], value_rows], 0)
    padded = jnp.concatenate(
        [
            jnp.zeros((1, local_width), jnp.bfloat16),
            queries,
            jnp.zeros((lead_rows, local_width), jnp.bfloat16),
        ],
        0,
    )
    padded = padded.reshape(spans_here + 1, SPAN, local_width)
    mixed = attend(padded, all_keys, all_values).reshape(-1, local_width)
    attended = mixed[1 : tok_rows + 1]
    partial_value = jnp.dot(attended, out_full, preferred_element_type=jnp.float32)
    summed = lax.psum_scatter(
        partial_value.astype(jnp.bfloat16), "db", scatter_dimension=1, tiled=True
    ).astype(jnp.float32)
    block = stream.astype(jnp.float32) + summed
    dense = dwa_weights[-1] * block + jnp.sum(
        history.astype(jnp.float32) * dwa_weights[:-1, None, None], axis=0
    )
    return (block.astype(jnp.bfloat16), dense.astype(jnp.bfloat16))


def solution(mesh):
    placed = (
        P("ctx", "db"),
        P(None, "ctx", "db"),
        P(),
        P("ctx", "db"),
        P("db", "ctx"),
        P("db", None, "ctx", None, None),
        P(),
    )
    return jax.shard_map(
        on_device,
        mesh=mesh,
        in_specs=placed,
        out_specs=(P("ctx", "db"), P("ctx", "db")),
        check_vma=False,
    )
```

profile of v0, /device:TPU:4, one launch (start us, length us, event | category | flops | bytes accessed | tf_op | source)
XLA Modules:
  0.0 305.9 jit_solution(4108286600987173053)
XLA Ops:
  7.2 0.7 all-gather.6.cloned.1.call-update
  7.9 0.7 all-gather.4.cloned.1.call-update
  8.6 13.2 %copy.54 = bf16[1,24,4,2,4096]{1,2,3,0,4:T(4,128)(2,1)} copy(bf16[1,24,4,2,4096]{4,3,2,1,0:T(2,128)(2,1)} %param.12) | data formatting | bytes 3145728 | tf_op args[5]
  21.8 12.7 %reshape.48 = bf16[16,2,24576]{2,1,0:T(2,128)(2,1)} reshape(bf16[4096,1,2,4,24]{4,3,2,1,0:T(4,128)(2,1)} %bitcast.32) | data formatting | bytes 3145728
  34.6 10.6 %all-to-all-start = ((bf16[16,2,24576]{2,1,0:T(2,128)(2,1)}), bf16[16,2,24576]{2,1,0:T(2,128)(2,1)S(1)}, u32[]{:S(2)}, u32[]{:S(2)}) async-start(bf16[16,2,24576]{2,1,0:T(2,128)(2,1)} %reshape.48), calls=%async_computation | async-start | bytes 3145728 | tf_op jit(solution)/shard_map/all_to_all | solution.py:45
  45.5 37.5 %all-to-all-done = bf16[16,2,24576]{2,1,0:T(2,128)(2,1)S(1)} async-done(((bf16[16,2,24576]{2,1,0:T(2,128)(2,1)}), bf16[16,2,24576]{2,1,0:T(2,128)(2,1)S(1)}, u32[]{:S(2)}, u32[]{:S(2)}) %all-to-all-start) | async-done | bytes 1572896 | tf_op jit(solution)/shard_map/all_to_all | solution.py:45
  83.0 12.9 %reshape.49 = bf16[4096,1,2,4,24]{4,3,2,1,0:T(4,128)(2,1)} reshape(bf16[16,2,24576]{2,1,0:T(2,128)(2,1)S(1)} %all-to-all-done) | data formatting | bytes 3145728
  95.8 10.8 %copy.73 = bf16[1,24,4,2,16,256]{5,1,4,3,2,0:T(8,128)(2,1)S(1)} copy(bf16[1,24,4,2,16,256]{1,2,3,5,4,0:T(4,128)(2,1)} %bitcast.31) | data formatting | bytes 3145728 | tf_op jit(solution)/shard_map/all_to_all | solution.py:45
  106.6 1.2 copy.58
  107.9 3.2 %gather_fusion = bf16[384,4,2,256]{3,1,2,0:T(4,128)(2,1)S(1)} fusion(bf16[384,4,2,256]{3,1,2,0:T(4,128)(2,1)S(1)} %copy.58, s32[1024]{0:T(1024)S(1)} %pad_clamp_fusion), kind=kCustom, calls=%fused_computation | custom fusion | bytes 3147264 | tf_op jit(solution)/shard_map/jit(_take)/gather | solution.py:51
  111.0 3.0 broadcast_select_fusion
  114.0 10.2 %all-to-all-start.1 = ((bf16[12,32,4,2,256]{4,3,2,0,1:T(2,128)(2,1)}), bf16[12,32,4,2,256]{4,3,2,0,1:T(2,128)(2,1)S(1)}, u32[]{:S(2)}, u32[]{:S(2)}) async-start(bf16[12,32,4,2,256]{4,3,2,0,1:T(2,128)(2,1)} %broadcast_select_fusion), calls=%async_computation.1 | async-start | bytes 3145728 | tf_op jit(solution)/shard_map/all_to_all | solution.py:52
  124.3 0.7 all-gather.8.cloned.1.call-update
  125.1 21.3 %all-gather.4.cloned.1.call-done = bf16[384,4096]{1,0:T(8,128)(2,1)} async-done(((bf16[384,256]{1,0:T(8,128)(2,1)}), bf16[384,4096]{1,0:T(8,128)(2,1)}) %all-gather.4.cloned.1.call-update) | async-done | bytes 3145744 | tf_op jit(solution)/shard_map/all_gather | solution.py:38
  146.4 3.5 %convolution_convert_fusion.2 = bf16[384,256]{1,0:T(8,128)(2,1)S(1)} fusion(bf16[384,4096]{1,0:T(8,128)(2,1)} %all-gather.4.cloned.1.call-done, bf16[4096,256]{1,0:T(8,128)(2,1)} %all-gather.6.cloned.1.call-done), kind=kOutput, calls=%fused_computation.9 | convolution fusion | flops 805404672 | bytes 5439488 | tf_op jit(solution)/shard_map/dot_general | solution.py:39
  150.1 0.8 reshape_reshape.6
  150.9 14.0 %all-to-all-done.1 = bf16[12,32,4,2,256]{4,3,2,0,1:T(2,128)(2,1)S(1)} async-done(((bf16[12,32,4,2,256]{4,3,2,0,1:T(2,128)(2,1)}), bf16[12,32,4,2,256]{4,3,2,0,1:T(2,128)(2,1)S(1)}, u32[]{:S(2)}, u32[]{:S(2)}) %all-to-all-start.1) | async-done | bytes 1572896 | tf_op jit(solution)/shard_map/all_to_all | solution.py:52
  165.1 0.9 copy.60
  166.0 2.1 collective-permute-start
  168.1 1.3 copy.62
  169.5 2.2 fusion.28
  171.7 2.6 copy.67
  174.3 1.5 copy.69
  175.8 0.9 copy.63
  178.0 1.5 fusion.30
  179.5 1.5 fusion.3
  181.3 46.6 %all-gather.8.cloned.1.call-done = bf16[256,4096]{1,0:T(8,128)(2,1)} async-done(((bf16[256,128]{1,0:T(8,128)(2,1)}), bf16[256,4096]{1,0:T(8,128)(2,1)}) %all-gather.8.cloned.1.call-update) | async-done | bytes 2097168 | tf_op jit(solution)/shard_map/all_gather | solution.py:44
  228.0 4.2 %convolution_convert_fusion = bf16[384,4096]{1,0:T(8,128)(2,1)} fusion(bf16[256,4096]{1,0:T(8,128)(2,1)} %all-gather.8.cloned.1.call-done, bf16[448,256]{1,0:T(8,128)(2,1)S(1)} %bitcast.38), kind=kOutput, calls=%fused_computation.2 | convolution fusion | flops 806879232 | bytes 5439488 | tf_op jit(solution)/shard_map/dot_general | solution.py:70
  232.2 0.6 copy-done.4
  232.8 0.6 slice.31
  234.0 63.0 %reduce-scatter.2.cloned.1.call-done = bf16[384,256]{1,0:T(8,128)(2,1)} async-done(((bf16[384,4096]{1,0:T(8,128)(2,1)}), bf16[384,256]{1,0:T(8,128)(2,1)}) %reduce-scatter.2.cloned.1.call-update) | async-done | bytes 196624 | tf_op jit(solution)/shard_map/reduce_scatter | solution.py:71
  297.0 2.4 add_convert_fusion
  (36 shorter events, 3.0 us)
Async XLA Ops:
  7.2 118.0 %all-gather.6.cloned.1.call-start = ((), (), s32[]{:S(2)}) async-start(), calls=%async_computation.4 | async-start | bytes 2162688 | tf_op jit(solution)/shard_map/all_gather | solution.py:41
  7.9 138.5 %all-gather.4.cloned.1.call-start = ((), (), s32[]{:S(2)}) async-start(), calls=%async_computation.3 | async-start | bytes 3342336 | tf_op jit(solution)/shard_map/all_gather | solution.py:38
  34.6 10.6 %copy-start.3 = (s32[384]{0:T(512)S(1)}, s32[384]{0:T(512)}, u32[]{:S(2)}) copy-start(s32[384]{0:T(512)} %param.13) | copy-start | bytes 4612
  34.6 48.4 %all-to-all-start = ((bf16[16,2,24576]{2,1,0:T(2,128)(2,1)}), bf16[16,2,24576]{2,1,0:T(2,128)(2,1)S(1)}, u32[]{:S(2)}, u32[]{:S(2)}) async-start(bf16[16,2,24576]{2,1,0:T(2,128)(2,1)} %reshape.48), calls=%async_computation | async-start | bytes 3145728 | tf_op jit(solution)/shard_map/all_to_all | solution.py:45
  114.0 50.9 %all-to-all-start.1 = ((bf16[12,32,4,2,256]{4,3,2,0,1:T(2,128)(2,1)}), bf16[12,32,4,2,256]{4,3,2,0,1:T(2,128)(2,1)S(1)}, u32[]{:S(2)}, u32[]{:S(2)}) async-start(bf16[12,32,4,2,256]{4,3,2,0,1:T(2,128)(2,1)} %broadcast_select_fusion), calls=%async_computation.1 | async-start | bytes 3145728 | tf_op jit(solution)/shard_map/all_to_all | solution.py:52
  124.2 103.7 %all-gather.8.cloned.1.call-start = ((), (), s32[]{:S(2)}) async-start(), calls=%async_computation.5 | async-start | bytes 2162688 | tf_op jit(solution)/shard_map/all_gather | solution.py:44
  125.0 172.0 %reduce-scatter.2.cloned.1.call-start = ((), (), s32[]{:S(2)}) async-start(), calls=%async_computation.6 | async-start | bytes 3342336 | tf_op jit(solution)/shard_map/reduce_scatter | solution.py:71
  166.0 11.1 %collective-permute-start = (bf16[256,2,256]{2,1,0:T(2,128)(2,1)}, bf16[256,2,256]{2,1,0:T(2,128)(2,1)S(1)}, u32[]{:S(2)}, u32[]{:S(2)}) collective-permute-start(bf16[256,2,256]{2,1,0:T(2,128)(2,1)} %bitcast.6), channel_id=1, source_target_pairs={{0,16},{16,32},{32,48},{48,64},{64,80},{80,96},{96,112},{112,128},... | collective-permute-start | bytes 786440 | tf_op jit(solution)/shard_map/ppermute | solution.py:14
  177.1 0.9 copy-start.2
  232.2 0.7 copy-start.4
  232.2 1.4 copy-start
  232.8 64.2 %copy-start.1 = (bf16[384,256]{1,0:T(8,128)(2,1)S(1)}, bf16[384,256]{1,0:T(8,128)(2,1)}, u32[]{:S(2)}) copy-start(bf16[384,256]{1,0:T(8,128)(2,1)} %param.7) | copy-start | bytes 589828
Sparse Core Ops, SparseCore 0:
  11.1 86.3 all-gather.5
  99.6 46.7 all-gather.3
  149.4 78.4 all-gather.7
  232.3 64.6 reduce-scatter.1
where the time goes:
time: 307 us; the launch traced here: 306 us
  waiting for transfers between devices  185 us (60%)
  local copies, waits for them, and re-layouts  67.7 us (22%)
  starting transfers between devices  23.1 us (8%)
  between operations  14 us (5%)
  matrix products  10.7 us (3%)
  other arithmetic  5.92 us (2%)
    reduce_scatter x1, waiting for transfers between devices, on_device(): lax.psum_scatter(partial_value.astype(jnp.bfloat16), 'db', scatter_dimens...  63 us
    all_gather x1, waiting for transfers between devices, on_device(): out_full = lax.all_gather(w_out, 'ctx', axis=1, tiled=True)  46.6 us
    unnamed x14, local copies, waits for them, and re-layouts  39.6 us
    all_to_all x1, waiting for transfers between devices, on_device(): lax.all_to_all(encoded_kv, 'db', split_axis=4, concat_axis=0, tiled=True)  37.5 us
    all_gather x1, waiting for transfers between devices, on_device(): full_stream = lax.all_gather(stream, 'db', axis=1, tiled=True)  21.3 us
    all_to_all x1, waiting for transfers between devices, on_device(): lax.all_to_all(outgoing, 'ctx', split_axis=1, concat_axis=1, tiled=True)  14 us
    all_to_all x1, local copies, waits for them, and re-layouts, on_device(): lax.all_to_all(encoded_kv, 'db', split_axis=4, concat_axis=0, tiled=True)  10.8 us
    all_to_all x1, starting transfers between devices, on_device(): lax.all_to_all(encoded_kv, 'db', split_axis=4, concat_axis=0, tiled=True)  10.6 us
  transfers between devices with their start and end apart: 7, of which 5 were waited for; matrix products, arithmetic and copies ran while one was open for 25% of the time, Pallas kernels for 0%

commit v1 on v0

--- a/solution.py
+++ b/solution.py
@@ -35,7 +35,10 @@
     local_width = w_query.shape[1]
     spans_here = tok_rows // SPAN
     lead_rows = SPAN - 1
-    full_stream = lax.all_gather(stream, "db", axis=1, tiled=True)
+    _part_trails = lambda body: jnp.concatenate(
+        lax.all_to_all(jnp.stack(lax.axis_size("db") * [body], 0), "db", 0, 0), 1
+    )
+    full_stream = _part_trails(stream)
     queries = jnp.dot(
         full_stream,
         lax.all_gather(w_query, "ctx", axis=0, tiled=True),

time: 307 us -> 343 us (1.12)
  waiting for transfers between devices: 185 us -> 211 us
  starting transfers between devices: 23.1 us -> 29.4 us
    all_to_all x0 -> x1, waiting for transfers between devices: none -> 39.8 us  [on_device(): lax.all_to_all(jnp.stack(lax.axis_size('db') * [body], 0), 'db', 0, 0)]
    all_gather x1 -> x0, waiting for transfers between devices: 21.3 us -> none  [on_device(): full_stream = lax.all_gather(stream, 'db', axis=1, tiled=True)]
    all_to_all x1, waiting for transfers between devices: 14 us -> 27.4 us  [on_device(): lax.all_to_all(outgoing, 'ctx', split_axis=1, concat_axis=1, tiled=True)]
    all_gather x1, waiting for transfers between devices: 46.6 us -> 36 us  [on_device(): out_full = lax.all_gather(w_out, 'ctx', axis=1, tiled=True)]
    all_gather x1, waiting for transfers between devices: 0.01 us -> 6.08 us  [on_device(): lax.all_gather(w_query, 'ctx', axis=0, tiled=True)]
    all_to_all x0 -> x1, starting transfers between devices: none -> 4.97 us  [on_device(): lax.all_to_all(jnp.stack(lax.axis_size('db') * [body], 0), 'db', 0, 0)]
    unnamed x14 -> x17, local copies, waits for them, and re-layouts: 39.6 us -> 39.8 us
  transfers between devices with their start and end apart: 7 -> 7, of which waited for: 5 -> 6; matrix products, arithmetic and copies ran while one was open for 25% -> 15% of each run, Pallas kernels for 0% -> 0%
where the time goes in v1:
time: 343 us; the launch traced here: 341 us
  waiting for transfers between devices  211 us (62%)
  local copies, waits for them, and re-layouts  70 us (20%)
  starting transfers between devices  29.4 us (9%)
  between operations  14 us (4%)
  matrix products  10.8 us (3%)
  other arithmetic  5.92 us (2%)
    reduce_scatter x1, waiting for transfers between devices, on_device(): lax.psum_scatter(partial_value.astype(jnp.bfloat16), 'db', scatter_dimens...  63 us
    unnamed x17, local copies, waits for them, and re-layouts  39.8 us
    all_to_all x1, waiting for transfers between devices, on_device(): lax.all_to_all(jnp.stack(lax.axis_size('db') * [body], 0), 'db', 0, 0)  39.8 us
    all_to_all x1, waiting for transfers between devices, on_device(): lax.all_to_all(encoded_kv, 'db', split_axis=4, concat_axis=0, tiled=True)  37.7 us
    all_gather x1, waiting for transfers between devices, on_device(): out_full = lax.all_gather(w_out, 'ctx', axis=1, tiled=True)  36 us
    all_to_all x1, waiting for transfers between devices, on_device(): lax.all_to_all(outgoing, 'ctx', split_axis=1, concat_axis=1, tiled=True)  27.4 us
    all_to_all x1, local copies, waits for them, and re-layouts, on_device(): lax.all_to_all(encoded_kv, 'db', split_axis=4, concat_axis=0, tiled=True)  10.8 us
    all_to_all x1, starting transfers between devices, on_device(): lax.all_to_all(encoded_kv, 'db', split_axis=4, concat_axis=0, tiled=True)  10.6 us
  transfers between devices with their start and end apart: 7, of which 6 were waited for; matrix products, arithmetic and copies ran while one was open for 15% of the time, Pallas kernels for 0%

profile of v1, /device:TPU:4, one launch (start us, length us, event | category | flops | bytes accessed | tf_op | source)
XLA Modules:
  0.0 341.4 jit_solution(18300394118482292368)
XLA Ops:
  7.2 13.2 %copy.57 = bf16[1,24,4,2,4096]{1,2,3,0,4:T(4,128)(2,1)} copy(bf16[1,24,4,2,4096]{4,3,2,1,0:T(2,128)(2,1)} %param.12) | data formatting | bytes 3145728 | tf_op args[5]
  20.4 12.7 %reshape.58 = bf16[16,2,24576]{2,1,0:T(2,128)(2,1)} reshape(bf16[4096,1,2,4,24]{4,3,2,1,0:T(4,128)(2,1)} %bitcast.35) | data formatting | bytes 3145728
  33.1 10.6 %all-to-all-start = ((bf16[16,2,24576]{2,1,0:T(2,128)(2,1)}), bf16[16,2,24576]{2,1,0:T(2,128)(2,1)S(1)}, u32[]{:S(2)}, u32[]{:S(2)}) async-start(bf16[16,2,24576]{2,1,0:T(2,128)(2,1)} %reshape.58), calls=%async_computation | async-start | bytes 3145728 | tf_op jit(solution)/shard_map/all_to_all | solution.py:48
  43.8 37.7 %all-to-all-done = bf16[16,2,24576]{2,1,0:T(2,128)(2,1)S(1)} async-done(((bf16[16,2,24576]{2,1,0:T(2,128)(2,1)}), bf16[16,2,24576]{2,1,0:T(2,128)(2,1)S(1)}, u32[]{:S(2)}, u32[]{:S(2)}) %all-to-all-start) | async-done | bytes 1572896 | tf_op jit(solution)/shard_map/all_to_all | solution.py:48
  81.5 2.1 stack.2
  83.6 5.0 %all-to-all-start.2 = ((bf16[16,384,256]{1,2,0:T(8,128)(2,1)}), bf16[16,384,256]{1,2,0:T(8,128)(2,1)}, u32[]{:S(2)}, u32[]{:S(2)}) async-start(bf16[16,384,256]{1,2,0:T(8,128)(2,1)} %stack.2), calls=%async_computation.2 | async-start | bytes 6291456 | tf_op jit(solution)/shard_map/all_to_all | solution.py:39
  88.7 0.7 all-gather.3.cloned.1.call-update
  89.7 12.9 %reshape.59 = bf16[4096,1,2,4,24]{4,3,2,1,0:T(4,128)(2,1)} reshape(bf16[16,2,24576]{2,1,0:T(2,128)(2,1)S(1)} %all-to-all-done) | data formatting | bytes 3145728
  102.5 10.8 %copy.77 = bf16[1,24,4,2,16,256]{5,1,4,3,2,0:T(8,128)(2,1)S(1)} copy(bf16[1,24,4,2,16,256]{1,2,3,5,4,0:T(4,128)(2,1)} %bitcast.34) | data formatting | bytes 3145728 | tf_op jit(solution)/shard_map/all_to_all | solution.py:48
  113.4 1.2 copy.61
  114.6 3.2 gather_fusion
  117.7 3.0 broadcast_select_fusion
  120.7 39.8 %all-to-all-done.2 = bf16[16,384,256]{1,2,0:T(8,128)(2,1)} async-done(((bf16[16,384,256]{1,2,0:T(8,128)(2,1)}), bf16[16,384,256]{1,2,0:T(8,128)(2,1)}, u32[]{:S(2)}, u32[]{:S(2)}) %all-to-all-start.2) | async-done | bytes 3145760 | tf_op jit(solution)/shard_map/all_to_all | solution.py:39
  160.5 10.2 %all-to-all-start.1 = ((bf16[12,32,4,2,256]{4,3,2,0,1:T(2,128)(2,1)}), bf16[12,32,4,2,256]{4,3,2,0,1:T(2,128)(2,1)S(1)}, u32[]{:S(2)}, u32[]{:S(2)}) async-start(bf16[12,32,4,2,256]{4,3,2,0,1:T(2,128)(2,1)} %broadcast_select_fusion), calls=%async_computation.1 | async-start | bytes 3145728 | tf_op jit(solution)/shard_map/all_to_all | solution.py:55
  170.8 0.7 all-gather.5.cloned.1.call-update
  171.6 6.1 %all-gather.3.cloned.1.call-done = bf16[4096,256]{1,0:T(8,128)(2,1)} async-done(((bf16[128,256]{1,0:T(8,128)(2,1)}), bf16[4096,256]{1,0:T(8,128)(2,1)}) %all-gather.3.cloned.1.call-update) | async-done | bytes 2097168 | tf_op jit(solution)/shard_map/all_gather | solution.py:44
  177.7 3.6 %convolution_convert_fusion.2 = bf16[384,256]{1,0:T(8,128)(2,1)S(1)} fusion(bf16[384,4096]{0,1:T(8,128)(2,1)} %bitcast.11, bf16[4096,256]{1,0:T(8,128)(2,1)} %all-gather.3.cloned.1.call-done), kind=kOutput, calls=%fused_computation.9 | convolution fusion | flops 805404672 | bytes 5439488 | tf_op jit(solution)/shard_map/dot_general | solution.py:42
  181.4 0.8 reshape_reshape.6
  182.2 27.4 %all-to-all-done.1 = bf16[12,32,4,2,256]{4,3,2,0,1:T(2,128)(2,1)S(1)} async-done(((bf16[12,32,4,2,256]{4,3,2,0,1:T(2,128)(2,1)}), bf16[12,32,4,2,256]{4,3,2,0,1:T(2,128)(2,1)S(1)}, u32[]{:S(2)}, u32[]{:S(2)}) %all-to-all-start.1) | async-done | bytes 1572896 | tf_op jit(solution)/shard_map/all_to_all | solution.py:55
  209.8 0.9 copy.63
  210.7 3.5 %collective-permute-start = (bf16[256,2,256]{2,1,0:T(2,128)(2,1)}, bf16[256,2,256]{2,1,0:T(2,128)(2,1)S(1)}, u32[]{:S(2)}, u32[]{:S(2)}) collective-permute-start(bf16[256,2,256]{2,1,0:T(2,128)(2,1)} %bitcast.6), channel_id=1, source_target_pairs={{0,16},{16,32},{32,48},{48,64},{64,80},{80,96},{96,112},{112,128},... | collective-permute-start | bytes 786440 | tf_op jit(solution)/shard_map/ppermute | solution.py:14
  214.3 1.3 copy.65
  215.6 2.2 fusion.28
  217.9 2.6 copy.71
  220.4 1.5 copy.73
  221.9 0.9 copy.66
  224.2 1.5 fusion.30
  225.7 1.5 fusion.3
  227.5 36.0 %all-gather.5.cloned.1.call-done = bf16[256,4096]{1,0:T(8,128)(2,1)} async-done(((bf16[256,128]{1,0:T(8,128)(2,1)}), bf16[256,4096]{1,0:T(8,128)(2,1)}) %all-gather.5.cloned.1.call-update) | async-done | bytes 2097168 | tf_op jit(solution)/shard_map/all_gather | solution.py:47
  263.5 4.2 %convolution_convert_fusion = bf16[384,4096]{1,0:T(8,128)(2,1)} fusion(bf16[256,4096]{1,0:T(8,128)(2,1)} %all-gather.5.cloned.1.call-done, bf16[448,256]{1,0:T(8,128)(2,1)S(1)} %bitcast.41), kind=kOutput, calls=%fused_computation.2 | convolution fusion | flops 806879232 | bytes 5439488 | tf_op jit(solution)/shard_map/dot_general | solution.py:73
  269.5 63.0 %reduce-scatter.2.cloned.1.call-done = bf16[384,256]{1,0:T(8,128)(2,1)} async-done(((bf16[384,4096]{1,0:T(8,128)(2,1)}), bf16[384,256]{1,0:T(8,128)(2,1)}) %reduce-scatter.2.cloned.1.call-update) | async-done | bytes 196624 | tf_op jit(solution)/shard_map/reduce_scatter | solution.py:74
  332.5 2.4 add_convert_fusion
  (39 shorter events, 4.4 us)
Async XLA Ops:
  33.1 10.6 %copy-start.1 = (bf16[384,256]{1,0:T(8,128)(2,1)S(1)}, bf16[384,256]{1,0:T(8,128)(2,1)}, u32[]{:S(2)}) copy-start(bf16[384,256]{1,0:T(8,128)(2,1)} %param.7) | copy-start | bytes 589828
  33.1 48.4 %all-to-all-start = ((bf16[16,2,24576]{2,1,0:T(2,128)(2,1)}), bf16[16,2,24576]{2,1,0:T(2,128)(2,1)S(1)}, u32[]{:S(2)}, u32[]{:S(2)}) async-start(bf16[16,2,24576]{2,1,0:T(2,128)(2,1)} %reshape.58), calls=%async_computation | async-start | bytes 3145728 | tf_op jit(solution)/shard_map/all_to_all | solution.py:48
  83.6 5.7 %copy-start.4 = (s32[384]{0:T(512)S(1)}, s32[384]{0:T(512)}, u32[]{:S(2)}) copy-start(s32[384]{0:T(512)} %param.13) | copy-start | bytes 4612
  83.6 76.8 %all-to-all-start.2 = ((bf16[16,384,256]{1,2,0:T(8,128)(2,1)}), bf16[16,384,256]{1,2,0:T(8,128)(2,1)}, u32[]{:S(2)}, u32[]{:S(2)}) async-start(bf16[16,384,256]{1,2,0:T(8,128)(2,1)} %stack.2), calls=%async_computation.2 | async-start | bytes 6291456 | tf_op jit(solution)/shard_map/all_to_all | solution.py:39
  88.6 89.1 %all-gather.3.cloned.1.call-start = ((), (), s32[]{:S(2)}) async-start(), calls=%async_computation.4 | async-start | bytes 2162688 | tf_op jit(solution)/shard_map/all_gather | solution.py:44
  160.5 49.2 %all-to-all-start.1 = ((bf16[12,32,4,2,256]{4,3,2,0,1:T(2,128)(2,1)}), bf16[12,32,4,2,256]{4,3,2,0,1:T(2,128)(2,1)S(1)}, u32[]{:S(2)}, u32[]{:S(2)}) async-start(bf16[12,32,4,2,256]{4,3,2,0,1:T(2,128)(2,1)} %broadcast_select_fusion), calls=%async_computation.1 | async-start | bytes 3145728 | tf_op jit(solution)/shard_map/all_to_all | solution.py:55
  170.7 92.7 %all-gather.5.cloned.1.call-start = ((), (), s32[]{:S(2)}) async-start(), calls=%async_computation.5 | async-start | bytes 2162688 | tf_op jit(solution)/shard_map/all_gather | solution.py:47
  171.5 161.0 %reduce-scatter.2.cloned.1.call-start = ((), (), s32[]{:S(2)}) async-start(), calls=%async_computation.6 | async-start | bytes 3342336 | tf_op jit(solution)/shard_map/reduce_scatter | solution.py:74
  210.7 12.5 %collective-permute-start = (bf16[256,2,256]{2,1,0:T(2,128)(2,1)}, bf16[256,2,256]{2,1,0:T(2,128)(2,1)S(1)}, u32[]{:S(2)}, u32[]{:S(2)}) collective-permute-start(bf16[256,2,256]{2,1,0:T(2,128)(2,1)} %bitcast.6), channel_id=1, source_target_pairs={{0,16},{16,32},{32,48},{48,64},{64,80},{80,96},{96,112},{112,128},... | collective-permute-start | bytes 786440 | tf_op jit(solution)/shard_map/ppermute | solution.py:14
  223.2 0.9 copy-start.3
  267.7 0.7 copy-start.5
  267.7 1.4 copy-start
  268.3 64.2 %copy-start.2 = (bf16[384,256]{1,0:T(8,128)(2,1)S(1)}, bf16[384,256]{1,0:T(8,128)(2,1)}, u32[]{:S(2)}) copy-start(bf16[384,256]{1,0:T(8,128)(2,1)} %param.7) | copy-start | bytes 589828
Sparse Core Ops, SparseCore 0:
  92.6 85.0 all-gather.2
  180.7 82.6 all-gather.4
  267.8 64.6 reduce-scatter.1
